TPU v7x, 512 devices: a whole 4x4x16 slice. The times are simulated.
512 devices in a mesh: rows: 128 (over y, x, z_lo), rep: 4 (over z_hi, core).
Axes of the slice: x: 4, y: 4, z: 16 (z_hi: 2, z_lo: 8; z = z_hi * 8 + z_lo), core: 2. Of those that a mesh axis runs over, the one named last changes fastest.
Arguments:
- covariates: bfloat16 [1048576, 128], P(('rows', 'rep')), may hold values from -6 to 6
- treated: int32 [1048576], P(('rows', 'rep')), may hold values 0 or 1
- landmarks: bfloat16 [1024, 128], P('rows'), may hold values from -6 to 6
- land_treat: bfloat16 [1024], P('rows'), may hold values from 0 to 1
Outputs:
- gram: float32 [1024, 512], P('rows')
- moment: float32 [1024], P('rows')
All inputs are finite; a program needn't handle non-finite values. No bound on the sum of `treated` on one device may be relied on, other than what follows from the above.
Results may differ from a plain program's by a relative error of at most 0.0034.
Values may be sent and summed in bfloat16 or wider, within the bound.
No kernel may reach another device: no remote copies, remote signals or barrier semaphores. Data moves between devices by JAX's collectives and lax.ppermute only.
A program may use at most 64 MiB of HBM per device.

v0:
```python
import jax
import jax.numpy as jnp
from jax import lax
from jax.sharding import PartitionSpec as P

PANELS = 2
gamma_rate = 0.03125


def on_device(covariates, treated, landmarks, land_treat):
    width = covariates.shape[1]
    total_rows = covariates.shape[0] * lax.axis_size("rows") * lax.axis_size("rep")
    all_land, all_treat = (
        lax.all_gather(landmarks, "rows", axis=0, tiled=True),
        lax.all_gather(land_treat, "rows", axis=0, tiled=True),
    )
    rows_f = covariates.astype(jnp.float32)
    sq_rows = jnp.sum(rows_f * rows_f, axis=1)[:, None]
    land_f = all_land.astype(jnp.float32)
    sq_land = jnp.sum(land_f * land_f, axis=1)
    lt_value = all_treat.astype(jnp.float32)
    on_one = jnp.exp(-0.5 * jnp.square(1.0 - lt_value))
    on_zero = jnp.exp(-0.5 * jnp.square(lt_value))
    is_treated = treated[:, None] == 1
    panel_size = all_land.shape[0] // PANELS
    gram_terms = []
    kern_terms = []
    for panel in range(PANELS):
        first = panel * panel_size
        block = all_land[first : first + panel_size]
        cross = lax.dot_general(
            covariates, block, (((1,), (1,)), ((), ())), preferred_element_type=jnp.float32
        )
        kern = jnp.exp(
            gamma_rate
            * (2.0 * width - sq_rows - sq_land[None, first : first + panel_size] + 2.0 * cross)
        )
        factor = jnp.where(
            is_treated,
            on_one[None, first : first + panel_size],
            on_zero[None, first : first + panel_size],
        )
        features = (kern * factor).astype(jnp.bfloat16)
        gram_part = lax.dot_general(
            features, features, (((0,), (0,)), ((), ())), preferred_element_type=jnp.float32
        )
        gram_terms.append(gram_part / total_rows)
        kern_terms.append(jnp.sum(kern, axis=0) / total_rows)
    gram_term = jnp.concatenate(gram_terms, axis=0)
    moment_term = (on_one - on_zero) * jnp.concatenate(kern_terms, axis=0)
    shares = (
        lax.psum_scatter(gram_term, "rows", scatter_dimension=0, tiled=True),
        lax.psum_scatter(moment_term, "rows", scatter_dimension=0, tiled=True),
    )
    gram_out, moment_out = lax.psum((shares[0], shares[1]), "rep")
    return (gram_out, moment_out)


def solution(mesh):
    in_specs = (P(("rows", "rep"), None), P(("rows", "rep")), P("rows", None), P("rows"))
    out_specs = (P("rows", None), P("rows"))
    return jax.shard_map(
        on_device, mesh=mesh, in_specs=in_specs, out_specs=out_specs, check_vma=False
    )
```

profile of v0, /device:TPU:1, one launch (start us, length us, event | category | flops | bytes accessed | tf_op | source)
XLA Modules:
  0.0 2144.9 jit_solution(338041234744841244)
XLA Ops:
  7.2 0.0 copy-start
  7.2 0.0 reduce-scatter.2.cloned.1.call-start
  7.2 0.7 broadcast_compare_fusion
  8.0 1.3 fusion.20
  10.0 0.8 dynamic-update-slice
  10.8 477.4 %all-reduce = bf16[1024]{0:T(1024)(128)(2,1)S(1)} all-reduce(bf16[1024]{0:T(1024)(128)(2,1)S(1)} %dynamic-update-slice), channel_id=1, replica_groups=mesh['rows'=128,'rep'=4] {'rows'}, use_global_device_ids=true, to_apply=%add | all-reduce | flops 1024 | bytes 4096
  488.3 1.4 multiply_reduce_fusion
  489.7 457.1 %all_gather.6 = bf16[1024,128]{1,0:T(8,128)(2,1)S(1)} all-gather(bf16[8,128]{1,0:T(8,128)(2,1)} %param.6), channel_id=1, replica_groups=mesh['rows'=128,'rep'=4] {'rows'}, dimensions={0}, use_global_device_ids=true | all-gather | bytes 264192 | tf_op jit(solution)/shard_map/all_gather | solution.py:14
  946.7 0.2 multiply_reduce_fusion.1
  947.0 2.2 fusion.22
  949.2 0.0 copy-done
  949.2 1.1 fusion.21
  950.4 2.0 fusion.8
  952.3 2.0 fusion.9
  954.3 1.5 pad_maximum_fusion
  955.9 0.0 reduce-scatter.2.cloned.1.call-update
  956.5 463.3 %all-reduce.1 = f32[1024]{0:T(1024)S(1)} all-reduce(f32[1024]{0:T(1024)S(1)} %get-tuple-element.12), channel_id=3, replica_groups=mesh['rows'=128,'rep'=4] {'rows'}, use_global_device_ids=true, to_apply=%region_6.7.clone | all-reduce | flops 1024 | bytes 8192
  1419.8 0.1 dynamic-slice.2
  1419.9 584.4 %reduce-scatter.2.cloned.1.call-done = f32[8,512]{1,0:T(8,128)} async-done(((f32[1024,512]{1,0:T(8,128)}), f32[8,512]{1,0:T(8,128)}) %reduce-scatter.2.cloned.1.call-update) | async-done | bytes 16400 | tf_op jit(solution)/shard_map/reduce_scatter | solution.py:52
  2004.3 133.8 %all-reduce.2 = (f32[8,512]{1,0:T(8,128)}, f32[8]{0:T(128)}) all-reduce(f32[8,512]{1,0:T(8,128)} %reduce-scatter.2.cloned.1.call-done, f32[8]{0:T(128)S(1)} %dynamic-slice.2), channel_id=1, replica_groups=mesh['rows'=128,'rep'=4] {'rep'}, use_global_device_ids=true, to_apply=%region_3.4 | all-reduce | flops 4104 | bytes 32832 | tf_op jit(solution)/shard_map/psum | solution.py:55
  (7 shorter events, 0.0 us)
Async XLA Ops:
  7.2 942.0 %copy-start = (bf16[2048,128]{1,0:T(8,128)(2,1)S(1)}, bf16[2048,128]{1,0:T(8,128)(2,1)}, u32[]{:S(2)}) copy-start(bf16[2048,128]{1,0:T(8,128)(2,1)} %param.4) | copy-start | bytes 1572868
  7.2 1997.1 %reduce-scatter.2.cloned.1.call-start = ((), (), s32[]{:S(2)}) async-start(), calls=%async_computation.1 | async-start | bytes 2113536 | tf_op jit(solution)/shard_map/reduce_scatter | solution.py:52
Sparse Core Ops, SparseCore 0:
  956.0 1048.2 reduce-scatter.1
where the time goes:
time: 2150 us; the launch traced here: 2140 us
  blocking collectives  1530 us (71%)
  waiting for transfers between devices  584 us (27%)
    unnamed x2, blocking collectives  941 us
    reduce_scatter x1, waiting for transfers between devices, on_device(): lax.psum_scatter(gram_term, 'rows', scatter_dimension=0, tiled=True)  584 us
    all_gather x1, blocking collectives, on_device(): lax.all_gather(landmarks, 'rows', axis=0, tiled=True)  457 us
    psum x1, blocking collectives, on_device(): gram_out, moment_out = lax.psum((shares[0], shares[1]), 'rep')  134 us
  transfers between devices with their start and end apart: 1, of which 1 were waited for; matrix products, arithmetic and copies ran while one was open for 0% of the time, Pallas kernels for 0%

commit v1 on v0

--- a/solution.py
+++ b/solution.py
@@ -7,11 +7,17 @@
 gamma_rate = 0.03125
 
 
+def solve_map(packet):
+    return jnp.concatenate(
+        lax.all_to_all(jnp.stack(lax.psum(1, "rows") * [packet]), "rows", 0, 0), 0
+    )
+
+
 def on_device(covariates, treated, landmarks, land_treat):
     width = covariates.shape[1]
     total_rows = covariates.shape[0] * lax.axis_size("rows") * lax.axis_size("rep")
     all_land, all_treat = (
-        lax.all_gather(landmarks, "rows", axis=0, tiled=True),
+        solve_map(landmarks),
         lax.all_gather(land_treat, "rows", axis=0, tiled=True),
     )
     rows_f = covariates.astype(jnp.float32)

time: 2150 us -> 1650 us (0.77)
  blocking collectives: 1530 us -> 1070 us
  waiting for transfers between devices: 584 us -> 528 us
    all_gather x1 -> x0, blocking collectives: 457 us -> none  [on_device(): lax.all_gather(landmarks, 'rows', axis=0, tiled=True)]
    reduce_scatter x1, waiting for transfers between devices: 584 us -> 528 us  [on_device(): lax.psum_scatter(gram_term, 'rows', scatter_dimension=0, tiled=True)]
  transfers between devices with their start and end apart: 1 -> 2, of which waited for: 1 -> 1; matrix products, arithmetic and copies ran while one was open for 0% -> 0% of each run, Pallas kernels for 0% -> 0%
where the time goes in v1:
time: 1650 us
  blocking collectives  1070 us (65%)
  waiting for transfers between devices  528 us (32%)
  starting transfers between devices  20.4 us (1%)
    unnamed x2, blocking collectives  936 us
    reduce_scatter x1, waiting for transfers between devices, on_device(): lax.psum_scatter(gram_term, 'rows', scatter_dimension=0, tiled=True)  528 us
    psum x1, blocking collectives, on_device(): gram_out, moment_out = lax.psum((shares[0], shares[1]), 'rep')  137 us
  transfers between devices with their start and end apart: 2, of which 1 were waited for; matrix products, arithmetic and copies ran while one was open for 0% of the time, Pallas kernels for 0%

profile of v1, /device:TPU:1, one launch (start us, length us, event | category | flops | bytes accessed | tf_op | source)
XLA Modules:
  0.0 1651.5 jit_solution(7145002999546787419)
XLA Ops:
  7.2 0.0 copy-start
  7.2 1.5 stack.2
  8.6 20.4 %all-to-all-start = ((bf16[128,8,128]{2,1,0:T(8,128)(2,1)}), bf16[128,8,128]{2,1,0:T(8,128)(2,1)S(1)}, u32[]{:S(2)}, u32[]{:S(2)}) async-start(bf16[128,8,128]{2,1,0:T(8,128)(2,1)} %stack.2), calls=%async_computation | async-start | bytes 524288 | tf_op jit(solution)/shard_map/all_to_all | solution.py:12
  29.0 0.0 reduce-scatter.2.cloned.1.call-start
  29.1 1.4 fusion.18
  31.1 0.8 dynamic-update-slice
  32.0 473.0 %all-reduce = bf16[1024]{0:T(1024)(128)(2,1)S(1)} all-reduce(bf16[1024]{0:T(1024)(128)(2,1)S(1)} %dynamic-update-slice), channel_id=1, replica_groups=mesh['rows'=128,'rep'=4] {'rows'}, use_global_device_ids=true, to_apply=%add | all-reduce | flops 1024 | bytes 4096
  504.9 1.4 multiply_reduce_fusion
  506.3 0.7 broadcast_compare_fusion
  507.0 0.0 all-to-all-done
  507.0 0.2 multiply_reduce_fusion.1
  507.3 0.1 sub.48
  507.4 0.1 sub.53
  507.4 2.2 fusion.19
  509.6 0.0 copy-done
  509.6 1.1 fusion.20
  510.8 2.0 fusion.8
  512.8 2.0 fusion.9
  514.8 1.5 pad_maximum_fusion
  516.3 0.0 reduce-scatter.2.cloned.1.call-update
  517.0 463.4 %all-reduce.1 = f32[1024]{0:T(1024)S(1)} all-reduce(f32[1024]{0:T(1024)S(1)} %get-tuple-element.12), channel_id=3, replica_groups=mesh['rows'=128,'rep'=4] {'rows'}, use_global_device_ids=true, to_apply=%region_6.7.clone | all-reduce | flops 1024 | bytes 8192
  980.3 0.1 dynamic-slice.2
  980.4 527.6 %reduce-scatter.2.cloned.1.call-done = f32[8,512]{1,0:T(8,128)} async-done(((f32[1024,512]{1,0:T(8,128)}), f32[8,512]{1,0:T(8,128)}) %reduce-scatter.2.cloned.1.call-update) | async-done | bytes 16400 | tf_op jit(solution)/shard_map/reduce_scatter | solution.py:58
  1508.0 136.7 %all-reduce.2 = (f32[8,512]{1,0:T(8,128)}, f32[8]{0:T(128)}) all-reduce(f32[8,512]{1,0:T(8,128)} %reduce-scatter.2.cloned.1.call-done, f32[8]{0:T(128)S(1)} %dynamic-slice.2), channel_id=1, replica_groups=mesh['rows'=128,'rep'=4] {'rep'}, use_global_device_ids=true, to_apply=%region_3.4 | all-reduce | flops 4104 | bytes 32832 | tf_op jit(solution)/shard_map/psum | solution.py:61
  (7 shorter events, 0.0 us)
Async XLA Ops:
  7.2 502.5 %copy-start = (bf16[2048,128]{1,0:T(8,128)(2,1)S(1)}, bf16[2048,128]{1,0:T(8,128)(2,1)}, u32[]{:S(2)}) copy-start(bf16[2048,128]{1,0:T(8,128)(2,1)} %param.4) | copy-start | bytes 1572868
  8.6 498.4 %all-to-all-start = ((bf16[128,8,128]{2,1,0:T(8,128)(2,1)}), bf16[128,8,128]{2,1,0:T(8,128)(2,1)S(1)}, u32[]{:S(2)}, u32[]{:S(2)}) async-start(bf16[128,8,128]{2,1,0:T(8,128)(2,1)} %stack.2), calls=%async_computation | async-start | bytes 524288 | tf_op jit(solution)/shard_map/all_to_all | solution.py:12
  29.0 1479.0 %reduce-scatter.2.cloned.1.call-start = ((), (), s32[]{:S(2)}) async-start(), calls=%async_computation.2 | async-start | bytes 2113536 | tf_op jit(solution)/shard_map/reduce_scatter | solution.py:58
Sparse Core Ops, SparseCore 0:
  516.5 991.4 reduce-scatter.1
